TPU v7x, 256 devices: a whole 4x4x8 slice. The times are simulated.
256 devices in a mesh: dp: 8 (over x, core), expert: 32 (over y, z).
Axes of the slice: x: 4, y: 4, z: 8, core: 2. Of those that a mesh axis runs over, the one named last changes fastest.
Arguments:
- tokens: bfloat16 [6144, 2048], P(('dp', 'expert')), may hold values from -6 to 6
- out_grad: bfloat16 [6144, 2048], P(('dp', 'expert')), may hold values from -0.59765625 to 0.59765625
- expert_ids: int32 [6144, 8], P(('dp', 'expert')), may hold values from 0 to 31, all different within a row; in each aligned block of 24 rows (0 to 23, 24 to 47, ...) at most 8 rows name the same one
- router_weight: bfloat16 [2048, 32], replicated, may hold values from -0.1875 to 0.1875
- w_gate: bfloat16 [32, 2048, 768], P('expert'), may hold values from -0.125 to 0.125
- w_up: bfloat16 [32, 2048, 768], P('expert'), may hold values from -0.125 to 0.125
- w_down: bfloat16 [32, 768, 2048], P('expert'), may hold values from -0.21875 to 0.21875
Outputs:
- grad_tokens: bfloat16 [6144, 2048], P(('dp', 'expert'))
- grad_router: float32 [2048, 32], replicated
- grad_gate: bfloat16 [32, 2048, 768], P('expert', 'dp')
- grad_up: bfloat16 [32, 2048, 768], P('expert', 'dp')
- grad_down: bfloat16 [32, 768, 2048], P('expert', 'dp')
Inputs may be any that keep to these rules, and one draw needn't show every extreme that they name: `expert_ids`: each row names 8 different experts. Among the 24 tokens of one device (aligned blocks of rows), no expert is named by more than 8 tokens, and in some blocks one expert is named by exactly 8.
All inputs are finite; a program needn't handle non-finite values.
Results may differ from a plain program's by a relative error of at most 0.017.
Values may be sent and summed in bfloat16 or wider, within the bound.
A program may use at most 128 MiB of HBM per device.

v0:
```python
import jax
import jax.numpy as jnp
from jax import lax
from jax.sharding import PartitionSpec as P

PASSES = 3


def expert_rows(rows_in, rows_grad, weight_gate, weight_up, weight_down):
    gate_pre = jnp.dot(rows_in, weight_gate, preferred_element_type=jnp.float32)
    up_pre = jnp.dot(rows_in, weight_up, preferred_element_type=jnp.float32)
    sigmoid_gate = jax.nn.sigmoid(gate_pre)
    activation = gate_pre * sigmoid_gate
    hidden = activation * up_pre
    contract_cols = (((1,), (1,)), ((), ()))
    hidden_grad = lax.dot_general(
        rows_grad, weight_down, contract_cols, preferred_element_type=jnp.float32
    )
    score_grad = jnp.sum(hidden_grad * hidden, axis=1).astype(jnp.bfloat16)
    gate_grad = (
        hidden_grad * up_pre * sigmoid_gate * (1.0 + gate_pre * (1.0 - sigmoid_gate))
    ).astype(jnp.bfloat16)
    up_grad = (hidden_grad * activation).astype(jnp.bfloat16)
    input_grad = lax.dot_general(
        gate_grad, weight_gate, contract_cols, preferred_element_type=jnp.float32
    )
    input_grad = input_grad + lax.dot_general(
        up_grad, weight_up, contract_cols, preferred_element_type=jnp.float32
    )
    return (
        hidden.astype(jnp.bfloat16),
        gate_grad,
        up_grad,
        input_grad.astype(jnp.bfloat16),
        score_grad,
    )


def scaled_rows(gate_values, rows_grad, gate_grad, up_grad):
    gate_scale = gate_values.astype(jnp.float32)[:, None]
    return (
        (gate_scale * rows_grad).astype(jnp.bfloat16),
        (gate_scale * gate_grad).astype(jnp.bfloat16),
        (gate_scale * up_grad).astype(jnp.bfloat16),
    )


def balancer_forward_pass(router_logit_rows):
    expert_density_rows = [jnp.exp(router_logit_rows)]
    division_ratios, column_totals, row_totals = ([], [], [])
    for repeat in range(PASSES):
        column_sum = lax.psum(jnp.sum(expert_density_rows[-1], axis=0), ("dp", "expert"))
        quotient = expert_density_rows[-1] / column_sum
        row_sum = jnp.sum(quotient, axis=1, keepdims=True)
        expert_density_rows.append(quotient / row_sum)
        division_ratios.append(quotient)
        column_totals.append(column_sum)
        row_totals.append(row_sum)
    return (expert_density_rows, division_ratios, column_totals, row_totals)


def balancer_adjoint_pass(
    density_gradient, expert_density_rows, division_ratios, column_totals, row_totals
):
    for repeat in reversed(range(PASSES)):
        density = expert_density_rows[repeat + 1]
        quotient_grad = (
            density_gradient - jnp.sum(density_gradient * density, axis=1, keepdims=True)
        ) / row_totals[repeat]
        shared = lax.psum(
            jnp.sum(quotient_grad * division_ratios[repeat], axis=0), ("dp", "expert")
        )
        density_gradient = (quotient_grad - shared) / column_totals[repeat]
    return density_gradient * expert_density_rows[0]


def column_product(operand_left, operand_right):
    return lax.dot_general(
        operand_left, operand_right, (((0,), (0,)), ((), ())), preferred_element_type=jnp.float32
    )


def per_device(tokens, out_grad, expert_ids, router_weight, w_gate, w_up, w_down):
    tok_rows, model_width = tokens.shape
    expert_blocks = router_weight.shape[1]
    top_picks = expert_ids.shape[1]
    capacity = min(tok_rows, 4 * tok_rows * top_picks // (3 * expert_blocks))
    sources = lax.axis_size("expert")
    slot_total = sources * capacity
    weight_gate, weight_up, weight_down = (w_gate[0], w_up[0], w_down[0])
    ff_width = weight_gate.shape[1]
    highest = lax.Precision.HIGHEST
    router_logit_rows = jnp.dot(tokens, router_weight, preferred_element_type=jnp.float32)
    expert_range = jnp.arange(expert_blocks, dtype=jnp.int32)
    picked = jnp.sum(
        (expert_ids[:, :, None] == expert_range[None, None, :]).astype(jnp.int32), axis=1
    )
    slot_rank = jnp.cumsum(picked, axis=0) - picked
    slot_range = jnp.arange(capacity, dtype=jnp.int32)
    selected = (slot_rank.T[:, None, :] == slot_range[None, :, None]) & (picked.T[:, None, :] > 0)
    select_half = selected.astype(jnp.bfloat16)
    select_full = selected.astype(jnp.float32)
    send_in = jnp.einsum(
        "ect,td->ecd", select_half, tokens, preferred_element_type=jnp.float32
    ).astype(jnp.bfloat16)
    send_grad = jnp.einsum(
        "ect,td->ecd", select_half, out_grad, preferred_element_type=jnp.float32
    ).astype(jnp.bfloat16)
    balancer_state = balancer_forward_pass(router_logit_rows)
    gate_matrix = expert_blocks * balancer_state[0][-1]
    send_gates = jnp.einsum("ect,te->ec", select_full, gate_matrix, precision=highest).astype(
        jnp.bfloat16
    )
    recv_in, recv_grad, recv_gates = (
        lax.all_to_all(send_in, "expert", split_axis=0, concat_axis=0, tiled=True),
        lax.all_to_all(send_grad, "expert", split_axis=0, concat_axis=0, tiled=True),
        lax.all_to_all(send_gates, "expert", split_axis=0, concat_axis=0, tiled=True),
    )
    flat_in = recv_in.reshape(slot_total, model_width)
    flat_grad = recv_grad.reshape(slot_total, model_width)
    hidden, gate_grad, up_grad, input_grad, score_grad = expert_rows(
        flat_in, flat_grad, weight_gate, weight_up, weight_down
    )
    input_slots, score_slots = (input_grad, score_grad)
    back_input, back_score = (
        lax.all_to_all(
            input_slots.reshape(sources, capacity, model_width),
            "expert",
            split_axis=0,
            concat_axis=0,
            tiled=True,
        ),
        lax.all_to_all(
            score_slots.reshape(sources, capacity),
            "expert",
            split_axis=0,
            concat_axis=0,
            tiled=True,
        ),
    )
    gate_values = recv_gates.reshape(slot_total)
    down_scaled, gate_scaled, up_scaled = scaled_rows(gate_values, flat_grad, gate_grad, up_grad)
    paired = jnp.concatenate([gate_scaled, up_scaled], axis=1)
    grad_pair = lax.psum_scatter(
        column_product(flat_in, paired).astype(jnp.bfloat16), "dp", scatter_dimension=0, tiled=True
    ).astype(jnp.float32)
    grad_down = lax.psum_scatter(
        column_product(hidden, down_scaled).astype(jnp.bfloat16),
        "dp",
        scatter_dimension=0,
        tiled=True,
    ).astype(jnp.float32)
    grad_gate = grad_pair[:, :ff_width].astype(jnp.bfloat16)[None]
    grad_up = grad_pair[:, ff_width:].astype(jnp.bfloat16)[None]
    grad_down = grad_down.astype(jnp.bfloat16)[None]
    route_weights = select_full * gate_matrix.T[:, None, :]
    expert_input = jnp.einsum(
        "ect,ecd->td", route_weights, back_input.astype(jnp.float32), precision=highest
    )
    density_gradient = expert_blocks * jnp.einsum(
        "ect,ec->te", select_full, back_score.astype(jnp.float32), precision=highest
    )
    expert_density_rows, division_ratios, column_totals, row_totals = balancer_state
    logit_gradient = balancer_adjoint_pass(
        density_gradient, expert_density_rows, division_ratios, column_totals, row_totals
    ).astype(jnp.bfloat16)
    router_term = lax.dot_general(
        tokens, logit_gradient, (((0,), (0,)), ((), ())), preferred_element_type=jnp.float32
    )
    grad_router = lax.psum(router_term, ("dp", "expert"))
    router_input = lax.dot_general(
        logit_gradient, router_weight, (((1,), (1,)), ((), ())), preferred_element_type=jnp.float32
    )
    grad_tokens = (expert_input + router_input).astype(jnp.bfloat16)
    return (grad_tokens, grad_router, grad_gate, grad_up, grad_down)


def solution(mesh):
    in_specs = (
        P(("dp", "expert"), None),
        P(("dp", "expert"), None),
        P(("dp", "expert"), None),
        P(),
        P("expert", None, None),
        P("expert", None, None),
        P("expert", None, None),
    )
    out_specs = (
        P(("dp", "expert"), None),
        P(),
        P("expert", "dp", None),
        P("expert", "dp", None),
        P("expert", "dp", None),
    )
    return jax.shard_map(
        per_device, mesh=mesh, in_specs=in_specs, out_specs=out_specs, check_vma=False
    )
```

profile of v0, /device:TPU:2, one launch (start us, length us, event | category | flops | bytes accessed | tf_op | source)
XLA Modules:
  0.0 830.9 jit_solution(2231783137656285111)
XLA Ops:
  8.0 0.9 copy.34
  9.0 0.1 convert_reduce_fusion
  9.1 1.1 fusion.58
  10.2 78.7 %psum.49 = f32[32]{0:T(128)S(1)} all-reduce(f32[32]{0:T(128)S(1)} %get-tuple-element.16), channel_id=1, replica_groups=mesh['dp'=8,'expert'=32] {'dp','expert'}, use_global_device_ids=true, to_apply=%region_3.4 | all-reduce | flops 32 | bytes 256 | tf_op jit(solution)/shard_map/psum | solution.py:52
  88.9 0.1 fusion.49
  89.0 0.1 fusion.50
  89.2 73.4 %psum.50 = f32[32]{0:T(128)S(1)} all-reduce(f32[32]{0:T(128)S(1)} %fusion.50), channel_id=1, replica_groups=mesh['dp'=8,'expert'=32] {'dp','expert'}, use_global_device_ids=true, to_apply=%region_6.7 | all-reduce | flops 32 | bytes 256 | tf_op jit(solution)/shard_map/psum | solution.py:52
  162.6 0.2 fusion.53
  162.8 0.1 fusion.54
  162.9 74.2 %psum.51 = f32[32]{0:T(128)S(1)} all-reduce(f32[32]{0:T(128)S(1)} %fusion.54), channel_id=1, replica_groups=mesh['dp'=8,'expert'=32] {'dp','expert'}, use_global_device_ids=true, to_apply=%region_9.10 | all-reduce | flops 32 | bytes 256 | tf_op jit(solution)/shard_map/psum | solution.py:52
  237.1 0.2 fusion.55
  237.5 0.7 copy.40
  238.2 5.9 all-to-all-start.4
  244.1 0.1 copy.35
  244.2 2.3 convolution_convert_fusion.2
  246.5 7.3 all-to-all-done.4
  253.8 4.7 all-to-all-start.1
  258.5 1.4 convolution_convert_fusion.3
  259.9 25.6 %all-to-all-done.1 = bf16[32,8,2048]{2,1,0:T(8,128)(2,1)} async-done(((bf16[32,8,2048]{2,1,0:T(8,128)(2,1)}), bf16[32,8,2048]{2,1,0:T(8,128)(2,1)}, u32[]{:S(2)}, u32[]{:S(2)}) %all-to-all-start.1) | async-done | bytes 1048608 | tf_op jit(solution)/shard_map/all_to_all | solution.py:115
  285.6 5.3 all-to-all-start
  291.1 4.1 fusion.6
  295.1 22.0 %all-to-all-done = bf16[32,8,2048]{2,1,0:T(8,128)(2,1)} async-done(((bf16[32,8,2048]{2,1,0:T(8,128)(2,1)}), bf16[32,8,2048]{2,1,0:T(8,128)(2,1)}, u32[]{:S(2)}, u32[]{:S(2)}) %all-to-all-start) | async-done | bytes 1048608 | tf_op jit(solution)/shard_map/all_to_all | solution.py:116
  317.2 3.3 fusion.8
  320.5 3.6 multiply_convert_fusion.3
  324.1 5.7 convolution_convert_fusion
  329.9 0.1 convert_element_type.110
  330.0 14.7 %all_to_all.33 = bf16[32,1,8]{2,1,0:T(2,128)(2,1)S(1)} all-to-all(bf16[32,1,8]{2,1,0:T(2,128)(2,1)S(1)} %convert_element_type.110), channel_id=1, replica_groups=mesh['dp'=8,'expert'=32] {'expert'}, dimensions={0} | all-to-all | bytes 1024 | tf_op jit(solution)/shard_map/all_to_all | solution.py:133
  344.8 0.2 fusion.46
  345.0 0.1 multiply_reduce_fusion.5
  345.1 74.4 %psum.52 = f32[32]{0:T(128)S(1)} all-reduce(f32[32]{0:T(128)S(1)} %multiply_reduce_fusion.5), channel_id=1, replica_groups=mesh['dp'=8,'expert'=32] {'dp','expert'}, use_global_device_ids=true, to_apply=%region_14.15 | all-reduce | flops 32 | bytes 256 | tf_op jit(solution)/shard_map/psum | solution.py:70
  419.5 0.2 multiply_reduce_fusion.4
  419.7 0.1 multiply_reduce_fusion.3
  419.9 74.5 %psum.53 = f32[32]{0:T(128)S(1)} all-reduce(f32[32]{0:T(128)S(1)} %get-tuple-element.9), channel_id=1, replica_groups=mesh['dp'=8,'expert'=32] {'dp','expert'}, use_global_device_ids=true, to_apply=%region_17.18 | all-reduce | flops 32 | bytes 256 | tf_op jit(solution)/shard_map/psum | solution.py:70
  494.3 0.2 multiply_reduce_fusion.2
  494.5 0.1 multiply_reduce_fusion.1
  494.6 73.3 %psum.54 = f32[32]{0:T(128)S(1)} all-reduce(f32[32]{0:T(128)S(1)} %multiply_reduce_fusion.1), channel_id=1, replica_groups=mesh['dp'=8,'expert'=32] {'dp','expert'}, use_global_device_ids=true, to_apply=%region_20.21 | all-reduce | flops 32 | bytes 256 | tf_op jit(solution)/shard_map/psum | solution.py:70
  567.9 1.0 convolution_bitcast_fusion
  569.1 4.6 convolution_convert_fusion.1
  573.7 0.9 copy-done.5
  574.7 1.0 fusion
  575.8 2.0 fusion.16
  577.8 6.0 all-to-all-start.2
  584.0 28.7 %all-to-all-done.2 = bf16[32,8,2048]{2,1,0:T(8,128)(2,1)} async-done(((bf16[32,8,2048]{2,1,0:T(8,128)(2,1)}), bf16[32,8,2048]{2,1,0:T(8,128)(2,1)}, u32[]{:S(2)}, u32[]{:S(2)}) %all-to-all-start.2) | async-done | bytes 1048608 | tf_op jit(solution)/shard_map/all_to_all | solution.py:126
  612.7 2.4 convolution_bitcast_fusion.1
  615.1 0.9 fusion.19
  616.0 2.0 slice_bitcast_fusion
  618.1 203.8 %all-reduce.2.cloned.1.call-done = f32[2048,32]{0,1:T(8,128)} async-done(((f32[2048,32]{0,1:T(8,128)}), f32[2048,32]{0,1:T(8,128)}) %all-reduce.2.cloned.1.call-update) | async-done | bytes 262160 | tf_op jit(solution)/shard_map/psum | solution.py:170
  821.8 1.7 copy.56
  (79 shorter events, 0.9 us)
Async XLA Ops:
  8.0 312.5 %copy-start = (bf16[1,2048,768]{2,1,0:T(8,128)(2,1)S(1)}, bf16[1,2048,768]{2,1,0:T(8,128)(2,1)}, u32[]{:S(2)}) copy-start(bf16[1,2048,768]{2,1,0:T(8,128)(2,1)} %param.11) | copy-start | bytes 9437188
  8.0 250.5 %copy-start.12 = (bf16[24,2048]{1,0:T(8,128)(2,1)S(1)}, bf16[24,2048]{1,0:T(8,128)(2,1)}, u32[]{:S(2)}) copy-start(bf16[24,2048]{1,0:T(8,128)(2,1)} %param.8) | copy-start | bytes 294916
  89.0 478.9 %copy-start.10 = (f32[24]{0:T(128)}, f32[24]{0:T(128)S(1)}, u32[]{:S(2)}) copy-start(f32[24]{0:T(128)S(1)} %fusion.49) | copy-start | bytes 292
  89.2 255.6 %copy-start.8 = (s32[32,24]{0,1:T(8,128)}, s32[32,24]{0,1:T(8,128)S(1)}, u32[]{:S(2)}) copy-start(s32[32,24]{0,1:T(8,128)S(1)} %subtract_bitcast_fusion) | copy-start | bytes 9220
  162.6 405.3 %copy-start.13 = (f32[32]{0:T(128)}, f32[32]{0:T(128)S(1)}, u32[]{:S(2)}) copy-start(f32[32]{0:T(128)S(1)} %psum.50) | copy-start | bytes 388
  162.8 256.9 %copy-start.17 = (f32[24]{0:T(128)}, f32[24]{0:T(128)S(1)}, u32[]{:S(2)}) copy-start(f32[24]{0:T(128)S(1)} %fusion.53) | copy-start | bytes 292
  162.9 181.9 %copy-start.15 = (pred[32,24]{0,1:T(8,128)(4,1)}, pred[32,24]{0,1:T(8,128)(4,1)S(1)}, u32[]{:S(2)}) copy-start(pred[32,24]{0,1:T(8,128)(4,1)S(1)} %compare_bitcast_fusion) | copy-start | bytes 2308
  237.1 182.6 %copy-start.19 = (f32[32]{0:T(128)}, f32[32]{0:T(128)S(1)}, u32[]{:S(2)}) copy-start(f32[32]{0:T(128)S(1)} %psum.51) | copy-start | bytes 388
  237.3 182.4 %copy-start.21 = (f32[24]{0:T(128)}, f32[24]{0:T(128)S(1)}, u32[]{:S(2)}) copy-start(f32[24]{0:T(128)S(1)} %fusion.55) | copy-start | bytes 292
  238.2 15.6 %all-to-all-start.4 = ((bf16[32,1,8]{2,1,0:T(2,128)(2,1)}), bf16[32,1,8]{2,1,0:T(2,128)(2,1)S(1)}, u32[]{:S(2)}, u32[]{:S(2)}) async-start(bf16[32,1,8]{2,1,0:T(2,128)(2,1)} %copy.40), calls=%async_computation.4 | async-start | bytes 32768 | tf_op jit(solution)/shard_map/all_to_all | solution.py:117
  253.8 31.8 %all-to-all-start.1 = ((bf16[32,8,2048]{2,1,0:T(8,128)(2,1)}), bf16[32,8,2048]{2,1,0:T(8,128)(2,1)}, u32[]{:S(2)}, u32[]{:S(2)}) async-start(bf16[32,8,2048]{2,1,0:T(8,128)(2,1)} %convolution_convert_fusion.2), calls=%async_computation.1 | async-start | bytes 2097152 | tf_op jit(solution)/shard_map/all_to_all | solution.py:115
  285.6 31.6 %all-to-all-start = ((bf16[32,8,2048]{2,1,0:T(8,128)(2,1)}), bf16[32,8,2048]{2,1,0:T(8,128)(2,1)}, u32[]{:S(2)}, u32[]{:S(2)}) async-start(bf16[32,8,2048]{2,1,0:T(8,128)(2,1)} %convolution_convert_fusion.3), calls=%async_computation | async-start | bytes 2097152 | tf_op jit(solution)/shard_map/all_to_all | solution.py:116
  290.9 325.1 %reduce-scatter.3.cloned.1.call-start = ((), (), s32[]{:S(2)}) async-start(), calls=%async_computation.8 | async-start | bytes 7077888 | tf_op jit(solution)/shard_map/reduce_scatter | solution.py:144
  317.2 3.3 copy-start.29
  329.8 238.1 %copy-start.2 = (bf16[24,2048]{1,0:T(8,128)(2,1)S(1)}, bf16[24,2048]{1,0:T(8,128)(2,1)}, u32[]{:S(2)}) copy-start(bf16[24,2048]{1,0:T(8,128)(2,1)} %param.7) | copy-start | bytes 294916
  329.9 492.0 %all-reduce.2.cloned.1.call-start = ((), (), s32[]{:S(2)}) async-start(), calls=%async_computation.7 | async-start | bytes 524288 | tf_op jit(solution)/shard_map/psum | solution.py:170
  419.9 149.2 %copy-start.6 = (f32[24,32]{1,0:T(8,128)}, f32[24,32]{1,0:T(8,128)S(1)}, u32[]{:S(2)}) copy-start(f32[24,32]{1,0:T(8,128)S(1)} %get-tuple-element.10) | copy-start | bytes 9220
  494.3 74.7 %copy-start.23 = (f32[32]{0:T(128)}, f32[32]{0:T(128)S(1)}, u32[]{:S(2)}) copy-start(f32[32]{0:T(128)S(1)} %psum.53) | copy-start | bytes 388
  494.5 74.5 %copy-start.25 = (f32[24]{0:T(128)}, f32[24]{0:T(128)S(1)}, u32[]{:S(2)}) copy-start(f32[24]{0:T(128)S(1)} %multiply_reduce_fusion.2) | copy-start | bytes 292
  567.9 1.1 copy-start.27
  569.0 252.9 %reduce-scatter.5.cloned.1.call-start = ((), (), s32[]{:S(2)}) async-start(), calls=%async_computation.9 | async-start | bytes 3538944 | tf_op jit(solution)/shard_map/reduce_scatter | solution.py:147
  573.7 1.0 copy-start.5
  573.7 2.0 copy-start.1
  573.7 2.0 copy-start.4
  575.7 8.1 copy-start.11
  575.7 8.1 copy-start.14
  575.7 8.1 copy-start.18
  575.7 8.1 copy-start.20
  575.7 8.1 copy-start.22
  575.7 36.9 %copy-start.9 = (s32[32,24]{0,1:T(8,128)S(1)}, s32[32,24]{0,1:T(8,128)}, u32[]{:S(2)}) copy-start(s32[32,24]{0,1:T(8,128)} %copy-done.8) | copy-start | bytes 9220
  575.8 36.9 %copy-start.16 = (pred[32,24]{0,1:T(8,128)(4,1)S(1)}, pred[32,24]{0,1:T(8,128)(4,1)}, u32[]{:S(2)}) copy-start(pred[32,24]{0,1:T(8,128)(4,1)} %copy-done.15) | copy-start | bytes 2308
  577.8 37.3 %copy-start.3 = (bf16[2048,32]{0,1:T(8,128)(2,1)S(1)}, bf16[2048,32]{0,1:T(8,128)(2,1)}, u32[]{:S(2)}) copy-start(bf16[2048,32]{0,1:T(8,128)(2,1)} %param.10) | copy-start | bytes 393220
  577.8 37.3 %copy-start.7 = (f32[24,32]{1,0:T(8,128)S(1)}, f32[24,32]{1,0:T(8,128)}, u32[]{:S(2)}) copy-start(f32[24,32]{1,0:T(8,128)} %copy-done.6) | copy-start | bytes 9220
  577.8 37.3 %copy-start.24 = (f32[32]{0:T(128)S(1)}, f32[32]{0:T(128)}, u32[]{:S(2)}) copy-start(f32[32]{0:T(128)} %copy-done.23) | copy-start | bytes 388
  577.8 37.3 %copy-start.26 = (f32[24]{0:T(128)S(1)}, f32[24]{0:T(128)}, u32[]{:S(2)}) copy-start(f32[24]{0:T(128)} %copy-done.25) | copy-start | bytes 292
  577.8 37.3 %copy-start.28 = (f32[32]{0:T(128)S(1)}, f32[32]{0:T(128)}, u32[]{:S(2)}) copy-start(f32[32]{0:T(128)} %copy-done.27) | copy-start | bytes 388
  577.8 34.9 %all-to-all-start.2 = ((bf16[32,8,2048]{2,1,0:T(8,128)(2,1)}), bf16[32,8,2048]{2,1,0:T(8,128)(2,1)}, u32[]{:S(2)}, u32[]{:S(2)}) async-start(bf16[32,8,2048]{2,1,0:T(8,128)(2,1)} %fusion.16), calls=%async_computation.2 | async-start | bytes 2097152 | tf_op jit(solution)/shard_map/all_to_all | solution.py:126
Sparse Core Ops, SparseCore 0:
  330.0 40.7 reduce-scatter.2
  573.8 31.8 reduce-scatter.4
Sparse Core Ops, SparseCore 1:
  569.0 252.7 all-reduce.1
where the time goes:
time: 832 us; the launch traced here: 831 us
  blocking collectives  463 us (56%)
  waiting for transfers between devices  287 us (34%)
  matrix products  33.5 us (4%)
  starting transfers between devices  22 us (3%)
  between operations  15.9 us (2%)
    psum x3, blocking collectives, balancer_forward_pass(): lax.psum(jnp.sum(expert_density_rows[-1], axis=0), ('dp', 'expert'))  226 us
    psum x3, blocking collectives, balancer_adjoint_pass(): lax.psum(jnp.sum(quotient_grad * division_ratios[repeat], axis=0), ('dp',...  222 us
    psum x1, waiting for transfers between devices, per_device(): grad_router = lax.psum(router_term, ('dp', 'expert'))  204 us
    all_to_all x1, waiting for transfers between devices, per_device(): lax.all_to_all(input_slots.reshape(sources, capacity, model_width), 'expe...  28.7 us
    all_to_all x1, waiting for transfers between devices, per_device(): lax.all_to_all(send_in, 'expert', split_axis=0, concat_axis=0, tiled=True)  25.6 us
    all_to_all x1, waiting for transfers between devices, per_device(): lax.all_to_all(send_grad, 'expert', split_axis=0, concat_axis=0, tiled=True)  22 us
  transfers between devices with their start and end apart: 7, of which 5 were waited for; matrix products, arithmetic and copies ran while one was open for 3% of the time, Pallas kernels for 0%

commit v1 on v0

--- a/solution.py
+++ b/solution.py
@@ -167,7 +167,9 @@
     router_term = lax.dot_general(
         tokens, logit_gradient, (((0,), (0,)), ((), ())), preferred_element_type=jnp.float32
     )
-    grad_router = lax.psum(router_term, ("dp", "expert"))
+    grad_router = router_term
+    for axis in ("dp", "expert"):
+        grad_router = lax.psum(grad_router, axis)
     router_input = lax.dot_general(
         logit_gradient, router_weight, (((1,), (1,)), ((), ())), preferred_element_type=jnp.float32
     )

time: 832 us -> 868 us (1.043)
  waiting for transfers between devices: 287 us -> 317 us
    reduce_scatter x1, waiting for transfers between devices: 0.01 us -> 35.1 us  [per_device(): lax.psum_scatter(column_product(hidden, down_scaled).astype(jnp.bfloat16)...]
    psum x1 -> x2, waiting for transfers between devices: 204 us -> 201 us  [per_device(): grad_router = lax.psum(grad_router, axis)]
  transfers between devices with their start and end apart: 7 -> 8, of which waited for: 5 -> 7; matrix products, arithmetic and copies ran while one was open for 3% -> 3% of each run, Pallas kernels for 0% -> 0%
where the time goes in v1:
time: 868 us; the launch traced here: 863 us
  blocking collectives  462 us (53%)
  waiting for transfers between devices  317 us (37%)
  matrix products  34.1 us (4%)
  starting transfers between devices  26.3 us (3%)
  between operations  14.2 us (2%)
    psum x3, blocking collectives, balancer_forward_pass(): lax.psum(jnp.sum(expert_density_rows[-1], axis=0), ('dp', 'expert'))  226 us
    psum x3, blocking collectives, balancer_adjoint_pass(): lax.psum(jnp.sum(quotient_grad * division_ratios[repeat], axis=0), ('dp',...  221 us
    psum x2, waiting for transfers between devices, per_device(): grad_router = lax.psum(grad_router, axis)  201 us
    reduce_scatter x1, waiting for transfers between devices, per_device(): lax.psum_scatter(column_product(hidden, down_scaled).astype(jnp.bfloat16)...  35.1 us
    all_to_all x1, waiting for transfers between devices, per_device(): lax.all_to_all(input_slots.reshape(sources, capacity, model_width), 'expe...  26.4 us
    all_to_all x1, waiting for transfers between devices, per_device(): lax.all_to_all(send_in, 'expert', split_axis=0, concat_axis=0, tiled=True)  25.5 us
    all_to_all x1, waiting for transfers between devices, per_device(): lax.all_to_all(send_grad, 'expert', split_axis=0, concat_axis=0, tiled=True)  22 us
  transfers between devices with their start and end apart: 8, of which 7 were waited for; matrix products, arithmetic and copies ran while one was open for 3% of the time, Pallas kernels for 0%

profile of v1, /device:TPU:2, one launch (start us, length us, event | category | flops | bytes accessed | tf_op | source)
XLA Modules:
  0.0 862.9 jit_solution(16193722566653267792)
XLA Ops:
  7.2 0.9 copy.34
  8.1 0.1 convert_reduce_fusion
  8.2 1.1 fusion.58
  9.4 78.7 %psum.56 = f32[32]{0:T(128)S(1)} all-reduce(f32[32]{0:T(128)S(1)} %get-tuple-element.16), channel_id=1, replica_groups=mesh['dp'=8,'expert'=32] {'dp','expert'}, use_global_device_ids=true, to_apply=%region_3.4 | all-reduce | flops 32 | bytes 256 | tf_op jit(solution)/shard_map/psum | solution.py:52
  88.1 0.1 fusion.49
  88.3 73.4 %psum.57 = f32[32]{0:T(128)S(1)} all-reduce(f32[32]{0:T(128)S(1)} %fusion.50), channel_id=1, replica_groups=mesh['dp'=8,'expert'=32] {'dp','expert'}, use_global_device_ids=true, to_apply=%region_6.7 | all-reduce | flops 32 | bytes 256 | tf_op jit(solution)/shard_map/psum | solution.py:52
  161.7 0.2 fusion.53
  161.9 0.1 fusion.54
  162.0 74.2 %psum.58 = f32[32]{0:T(128)S(1)} all-reduce(f32[32]{0:T(128)S(1)} %fusion.54), channel_id=1, replica_groups=mesh['dp'=8,'expert'=32] {'dp','expert'}, use_global_device_ids=true, to_apply=%region_9.10 | all-reduce | flops 32 | bytes 256 | tf_op jit(solution)/shard_map/psum | solution.py:52
  236.2 0.2 fusion.55
  236.6 0.7 copy.40
  237.3 5.9 all-to-all-start.4
  243.2 0.1 copy.35
  243.3 2.3 convolution_convert_fusion.2
  245.6 7.3 all-to-all-done.4
  252.9 4.7 all-to-all-start.1
  257.6 1.5 convolution_convert_fusion.3
  259.1 25.5 %all-to-all-done.1 = bf16[32,8,2048]{2,1,0:T(8,128)(2,1)} async-done(((bf16[32,8,2048]{2,1,0:T(8,128)(2,1)}), bf16[32,8,2048]{2,1,0:T(8,128)(2,1)}, u32[]{:S(2)}, u32[]{:S(2)}) %all-to-all-start.1) | async-done | bytes 1048608 | tf_op jit(solution)/shard_map/all_to_all | solution.py:115
  284.6 5.3 all-to-all-start
  290.1 4.1 fusion.6
  294.2 22.0 %all-to-all-done = bf16[32,8,2048]{2,1,0:T(8,128)(2,1)} async-done(((bf16[32,8,2048]{2,1,0:T(8,128)(2,1)}), bf16[32,8,2048]{2,1,0:T(8,128)(2,1)}, u32[]{:S(2)}, u32[]{:S(2)}) %all-to-all-start) | async-done | bytes 1048608 | tf_op jit(solution)/shard_map/all_to_all | solution.py:116
  316.3 3.3 fusion.8
  319.6 3.9 multiply_convert_fusion.3
  323.6 14.7 %all_to_all.33 = bf16[32,1,8]{2,1,0:T(2,128)(2,1)S(1)} all-to-all(bf16[32,1,8]{2,1,0:T(2,128)(2,1)S(1)} %convert_element_type.110), channel_id=1, replica_groups=mesh['dp'=8,'expert'=32] {'expert'}, dimensions={0} | all-to-all | bytes 1024 | tf_op jit(solution)/shard_map/all_to_all | solution.py:133
  338.4 0.2 fusion.46
  338.6 0.1 multiply_reduce_fusion.5
  338.7 73.8 %psum.59 = f32[32]{0:T(128)S(1)} all-reduce(f32[32]{0:T(128)S(1)} %multiply_reduce_fusion.5), channel_id=1, replica_groups=mesh['dp'=8,'expert'=32] {'dp','expert'}, use_global_device_ids=true, to_apply=%region_14.15 | all-reduce | flops 32 | bytes 256 | tf_op jit(solution)/shard_map/psum | solution.py:70
  412.5 0.2 multiply_reduce_fusion.4
  412.7 0.1 multiply_reduce_fusion.3
  412.8 74.2 %psum.60 = f32[32]{0:T(128)S(1)} all-reduce(f32[32]{0:T(128)S(1)} %get-tuple-element.9), channel_id=1, replica_groups=mesh['dp'=8,'expert'=32] {'dp','expert'}, use_global_device_ids=true, to_apply=%region_17.18 | all-reduce | flops 32 | bytes 256 | tf_op jit(solution)/shard_map/psum | solution.py:70
  487.0 0.2 multiply_reduce_fusion.2
  487.3 73.3 %psum.61 = f32[32]{0:T(128)S(1)} all-reduce(f32[32]{0:T(128)S(1)} %multiply_reduce_fusion.1), channel_id=1, replica_groups=mesh['dp'=8,'expert'=32] {'dp','expert'}, use_global_device_ids=true, to_apply=%region_20.21 | all-reduce | flops 32 | bytes 256 | tf_op jit(solution)/shard_map/psum | solution.py:70
  560.6 1.0 convolution_bitcast_fusion
  561.7 0.2 reduce-scatter.3.cloned.1.call-start
  561.9 5.9 convolution_convert_fusion
  567.9 53.0 %all-reduce.3.cloned.1.call-done = f32[2048,32]{0,1:T(8,128)} async-done(((f32[2048,32]{0,1:T(8,128)}), f32[2048,32]{0,1:T(8,128)}) %all-reduce.3.cloned.1.call-update) | async-done | bytes 262160 | tf_op jit(solution)/shard_map/psum | solution.py:172
  621.0 4.6 convolution_convert_fusion.1
  625.6 0.9 copy-done.5
  626.6 1.0 fusion
  627.7 2.0 fusion.16
  629.7 10.1 %all-to-all-start.2 = ((bf16[32,8,2048]{2,1,0:T(8,128)(2,1)}), bf16[32,8,2048]{2,1,0:T(8,128)(2,1)}, u32[]{:S(2)}, u32[]{:S(2)}) async-start(bf16[32,8,2048]{2,1,0:T(8,128)(2,1)} %fusion.16), calls=%async_computation.2 | async-start | bytes 2097152 | tf_op jit(solution)/shard_map/all_to_all | solution.py:126
  640.0 26.4 %all-to-all-done.2 = bf16[32,8,2048]{2,1,0:T(8,128)(2,1)} async-done(((bf16[32,8,2048]{2,1,0:T(8,128)(2,1)}), bf16[32,8,2048]{2,1,0:T(8,128)(2,1)}, u32[]{:S(2)}, u32[]{:S(2)}) %all-to-all-start.2) | async-done | bytes 1048608 | tf_op jit(solution)/shard_map/all_to_all | solution.py:126
  666.4 2.4 convolution_bitcast_fusion.1
  668.9 0.9 fusion.19
  669.7 2.0 slice_bitcast_fusion
  671.8 147.8 %all-reduce.5.cloned.1.call-done = f32[2048,32]{0,1:T(8,128)} async-done(((f32[2048,32]{0,1:T(8,128)}), f32[2048,32]{0,1:T(8,128)}) %all-reduce.5.cloned.1.call-update) | async-done | bytes 262160 | tf_op jit(solution)/shard_map/psum | solution.py:172
  819.6 35.1 %reduce-scatter.5.cloned.1.call-done = bf16[96,2048]{1,0:T(8,128)(2,1)} async-done(((bf16[768,2048]{1,0:T(8,128)(2,1)}), bf16[96,2048]{1,0:T(8,128)(2,1)}) %reduce-scatter.5.cloned.1.call-update) | async-done | bytes 393232 | tf_op jit(solution)/shard_map/reduce_scatter | solution.py:147
  854.7 1.7 copy.57
  (82 shorter events, 1.2 us)
Async XLA Ops:
  7.2 312.4 %copy-start = (bf16[1,2048,768]{2,1,0:T(8,128)(2,1)S(1)}, bf16[1,2048,768]{2,1,0:T(8,128)(2,1)}, u32[]{:S(2)}) copy-start(bf16[1,2048,768]{2,1,0:T(8,128)(2,1)} %param.11) | copy-start | bytes 9437188
  7.2 250.4 %copy-start.12 = (bf16[24,2048]{1,0:T(8,128)(2,1)S(1)}, bf16[24,2048]{1,0:T(8,128)(2,1)}, u32[]{:S(2)}) copy-start(bf16[24,2048]{1,0:T(8,128)(2,1)} %param.8) | copy-start | bytes 294916
  88.2 472.5 %copy-start.10 = (f32[24]{0:T(128)}, f32[24]{0:T(128)S(1)}, u32[]{:S(2)}) copy-start(f32[24]{0:T(128)S(1)} %fusion.49) | copy-start | bytes 292
  88.3 250.0 %copy-start.8 = (s32[32,24]{0,1:T(8,128)}, s32[32,24]{0,1:T(8,128)S(1)}, u32[]{:S(2)}) copy-start(s32[32,24]{0,1:T(8,128)S(1)} %subtract_bitcast_fusion) | copy-start | bytes 9220
  161.7 398.9 %copy-start.13 = (f32[32]{0:T(128)}, f32[32]{0:T(128)S(1)}, u32[]{:S(2)}) copy-start(f32[32]{0:T(128)S(1)} %psum.57) | copy-start | bytes 388
  161.9 250.7 %copy-start.17 = (f32[24]{0:T(128)}, f32[24]{0:T(128)S(1)}, u32[]{:S(2)}) copy-start(f32[24]{0:T(128)S(1)} %fusion.53) | copy-start | bytes 292
  162.0 176.3 %copy-start.15 = (pred[32,24]{0,1:T(8,128)(4,1)}, pred[32,24]{0,1:T(8,128)(4,1)S(1)}, u32[]{:S(2)}) copy-start(pred[32,24]{0,1:T(8,128)(4,1)S(1)} %compare_bitcast_fusion) | copy-start | bytes 2308
  236.2 176.4 %copy-start.19 = (f32[32]{0:T(128)}, f32[32]{0:T(128)S(1)}, u32[]{:S(2)}) copy-start(f32[32]{0:T(128)S(1)} %psum.58) | copy-start | bytes 388
  236.4 176.2 %copy-start.21 = (f32[24]{0:T(128)}, f32[24]{0:T(128)S(1)}, u32[]{:S(2)}) copy-start(f32[24]{0:T(128)S(1)} %fusion.55) | copy-start | bytes 292
  237.3 15.6 %all-to-all-start.4 = ((bf16[32,1,8]{2,1,0:T(2,128)(2,1)}), bf16[32,1,8]{2,1,0:T(2,128)(2,1)S(1)}, u32[]{:S(2)}, u32[]{:S(2)}) async-start(bf16[32,1,8]{2,1,0:T(2,128)(2,1)} %copy.40), calls=%async_computation.4 | async-start | bytes 32768 | tf_op jit(solution)/shard_map/all_to_all | solution.py:117
  252.9 31.7 %all-to-all-start.1 = ((bf16[32,8,2048]{2,1,0:T(8,128)(2,1)}), bf16[32,8,2048]{2,1,0:T(8,128)(2,1)}, u32[]{:S(2)}, u32[]{:S(2)}) async-start(bf16[32,8,2048]{2,1,0:T(8,128)(2,1)} %convolution_convert_fusion.2), calls=%async_computation.1 | async-start | bytes 2097152 | tf_op jit(solution)/shard_map/all_to_all | solution.py:115
  284.6 31.6 %all-to-all-start = ((bf16[32,8,2048]{2,1,0:T(8,128)(2,1)}), bf16[32,8,2048]{2,1,0:T(8,128)(2,1)}, u32[]{:S(2)}, u32[]{:S(2)}) async-start(bf16[32,8,2048]{2,1,0:T(8,128)(2,1)} %convolution_convert_fusion.3), calls=%async_computation | async-start | bytes 2097152 | tf_op jit(solution)/shard_map/all_to_all | solution.py:116
  290.0 331.0 %all-reduce.3.cloned.1.call-start = ((), (), s32[]{:S(2)}) async-start(), calls=%async_computation.7 | async-start | bytes 524288 | tf_op jit(solution)/shard_map/psum | solution.py:172
  316.2 3.3 copy-start.29
  319.6 241.1 %copy-start.2 = (bf16[24,2048]{1,0:T(8,128)(2,1)S(1)}, bf16[24,2048]{1,0:T(8,128)(2,1)}, u32[]{:S(2)}) copy-start(bf16[24,2048]{1,0:T(8,128)(2,1)} %param.7) | copy-start | bytes 294916
  412.8 155.0 %copy-start.6 = (f32[24,32]{1,0:T(8,128)}, f32[24,32]{1,0:T(8,128)S(1)}, u32[]{:S(2)}) copy-start(f32[24,32]{1,0:T(8,128)S(1)} %get-tuple-element.10) | copy-start | bytes 9220
  487.0 80.8 %copy-start.23 = (f32[32]{0:T(128)}, f32[32]{0:T(128)S(1)}, u32[]{:S(2)}) copy-start(f32[32]{0:T(128)S(1)} %psum.60) | copy-start | bytes 388
  487.2 80.6 %copy-start.25 = (f32[24]{0:T(128)}, f32[24]{0:T(128)S(1)}, u32[]{:S(2)}) copy-start(f32[24]{0:T(128)S(1)} %multiply_reduce_fusion.2) | copy-start | bytes 292
  560.6 7.2 copy-start.27
  561.7 108.1 %reduce-scatter.3.cloned.1.call-start = ((), (), s32[]{:S(2)}) async-start(), calls=%async_computation.9 | async-start | bytes 7077888 | tf_op jit(solution)/shard_map/reduce_scatter | solution.py:144
  567.8 251.7 %all-reduce.5.cloned.1.call-start = ((), (), s32[]{:S(2)}) async-start(), calls=%async_computation.8 | async-start | bytes 524288 | tf_op jit(solution)/shard_map/psum | solution.py:172
  621.0 233.7 %reduce-scatter.5.cloned.1.call-start = ((), (), s32[]{:S(2)}) async-start(), calls=%async_computation.10 | async-start | bytes 3538944 | tf_op jit(solution)/shard_map/reduce_scatter | solution.py:147
  625.6 1.0 copy-start.5
  625.6 2.0 copy-start.1
  625.6 2.0 copy-start.4
  627.7 12.2 %copy-start.11 = (f32[24]{0:T(128)S(1)}, f32[24]{0:T(128)}, u32[]{:S(2)}) copy-start(f32[24]{0:T(128)} %copy-done.10) | copy-start | bytes 292
  627.7 12.2 %copy-start.14 = (f32[32]{0:T(128)S(1)}, f32[32]{0:T(128)}, u32[]{:S(2)}) copy-start(f32[32]{0:T(128)} %copy-done.13) | copy-start | bytes 388
  627.7 12.2 %copy-start.18 = (f32[24]{0:T(128)S(1)}, f32[24]{0:T(128)}, u32[]{:S(2)}) copy-start(f32[24]{0:T(128)} %copy-done.17) | copy-start | bytes 292
  627.7 12.2 %copy-start.20 = (f32[32]{0:T(128)S(1)}, f32[32]{0:T(128)}, u32[]{:S(2)}) copy-start(f32[32]{0:T(128)} %copy-done.19) | copy-start | bytes 388
  627.7 12.2 %copy-start.22 = (f32[24]{0:T(128)S(1)}, f32[24]{0:T(128)}, u32[]{:S(2)}) copy-start(f32[24]{0:T(128)} %copy-done.21) | copy-start | bytes 292
  627.7 38.7 %copy-start.9 = (s32[32,24]{0,1:T(8,128)S(1)}, s32[32,24]{0,1:T(8,128)}, u32[]{:S(2)}) copy-start(s32[32,24]{0,1:T(8,128)} %copy-done.8) | copy-start | bytes 9220
  627.7 38.7 %copy-start.16 = (pred[32,24]{0,1:T(8,128)(4,1)S(1)}, pred[32,24]{0,1:T(8,128)(4,1)}, u32[]{:S(2)}) copy-start(pred[32,24]{0,1:T(8,128)(4,1)} %copy-done.15) | copy-start | bytes 2308
  629.7 39.1 %copy-start.3 = (bf16[2048,32]{0,1:T(8,128)(2,1)S(1)}, bf16[2048,32]{0,1:T(8,128)(2,1)}, u32[]{:S(2)}) copy-start(bf16[2048,32]{0,1:T(8,128)(2,1)} %param.10) | copy-start | bytes 393220
  629.7 39.1 %copy-start.7 = (f32[24,32]{1,0:T(8,128)S(1)}, f32[24,32]{1,0:T(8,128)}, u32[]{:S(2)}) copy-start(f32[24,32]{1,0:T(8,128)} %copy-done.6) | copy-start | bytes 9220
  629.7 39.1 %copy-start.24 = (f32[32]{0:T(128)S(1)}, f32[32]{0:T(128)}, u32[]{:S(2)}) copy-start(f32[32]{0:T(128)} %copy-done.23) | copy-start | bytes 388
  629.7 39.1 %copy-start.26 = (f32[24]{0:T(128)S(1)}, f32[24]{0:T(128)}, u32[]{:S(2)}) copy-start(f32[24]{0:T(128)} %copy-done.25) | copy-start | bytes 292
  629.7 39.1 %copy-start.28 = (f32[32]{0:T(128)S(1)}, f32[32]{0:T(128)}, u32[]{:S(2)}) copy-start(f32[32]{0:T(128)} %copy-done.27) | copy-start | bytes 388
  629.7 36.7 %all-to-all-start.2 = ((bf16[32,8,2048]{2,1,0:T(8,128)(2,1)}), bf16[32,8,2048]{2,1,0:T(8,128)(2,1)}, u32[]{:S(2)}, u32[]{:S(2)}) async-start(bf16[32,8,2048]{2,1,0:T(8,128)(2,1)} %fusion.16), calls=%async_computation.2 | async-start | bytes 2097152 | tf_op jit(solution)/shard_map/all_to_all | solution.py:126
Sparse Core Ops, SparseCore 0:
  561.8 59.0 all-reduce.2
  623.5 44.3 reduce-scatter.2
  671.4 148.1 all-reduce.4
  822.6 32.0 reduce-scatter.4
